TPU v7x, 32 devices: a whole 2x2x4 slice. The times are simulated.
32 devices in a mesh: clip: 2 (over x), slab: 16 (over z, y, core).
Axes of the slice: x: 2, y: 2, z: 4, core: 2. Of those that a mesh axis runs over, the one named last changes fastest.
Arguments:
- mask_field: float32 [4096, 2048], P(('clip', 'slab')), parts along dimension 0, may hold values from -1.8 to 2.9
- target_print: int32 [4096, 2048], P(('clip', 'slab')), parts along dimension 0, may hold values from 0 to 1
- source_points: int32 [32, 2], P('clip'), parts along dimension 0, may hold values from 0 to 60
- source_groups: int32 [32], P('clip'), parts along dimension 0, may hold values from 0 to 7
- group_logits: float32 [16], P('clip'), parts along dimension 0, may hold values from -1 to 1
- pupil_radius: int32 [2], P('clip'), parts along dimension 0, may hold values from 32 to 127
Outputs:
- loss_value: float32 [2], P('clip'), parts along dimension 0
- mask_grad: float32 [4096, 2048], P(('clip', 'slab')), parts along dimension 0
- group_grad: float32 [16], P('clip'), parts along dimension 0
There are 2 independent parts, one for each index of `clip`. A program takes and returns all parts, laid end to end along the dimension named above; each array names one. Nothing has to cross between parts.
All inputs are finite; a program needn't handle non-finite values.
Results may differ from a plain program's by a relative error of at most 0.0003.
Values sent between devices are 32-bit elements; how exact they have to be, the bound alone decides.
A program may use at most 128 MiB of HBM per device.

v0:
```python
import math
import jax
import jax.numpy as jnp
from jax import lax
from jax.sharding import PartitionSpec as P

K = 256
GRID = 61
NG = 8
steepness = 8.0
threshold = 0.3
shift_scale = 45
full_turn = 2.0 * math.pi
highest = lax.Precision.HIGHEST


def contract(form, left, right):
    return jnp.einsum(form, left, right, precision=highest)


def turn_table(left, right, length):
    product = jnp.mod(left[:, None] * right[None, :], length)
    angles = full_turn * product.astype(jnp.float32) / length
    return (jnp.cos(angles), jnp.sin(angles))


def pupil_mask(shifted, radius_sq, along_first, along_second):
    first_axis = along_first[None, :, None] + shifted[:, 0, None, None]
    second_axis = along_second[None, None, :] + shifted[:, 1, None, None]
    return (first_axis * first_axis + second_axis * second_axis <= radius_sq).astype(jnp.float32)


def on_device(mask_field, target_print, source_points, source_groups, group_logits, pupil_radius):
    row_count = mask_field.shape[0]
    length = mask_field.shape[1]
    half_band = K // 2
    device = lax.axis_index("slab")
    positions = device * row_count + jnp.arange(row_count, dtype=jnp.int32)
    everywhere = jnp.arange(length, dtype=jnp.int32)
    frequency = jnp.arange(K, dtype=jnp.int32) - half_band
    cos_full, sin_full = turn_table(everywhere, frequency, length)
    cos_local, sin_local = turn_table(positions, frequency, length)
    cutoff = pupil_radius[0]
    radius_sq = cutoff * cutoff
    shifted = (source_points - GRID // 2) * cutoff // shift_scale
    norming = 1.0 / (length * length)
    row_real = jnp.dot(mask_field, cos_full, precision=highest)
    row_imag = -jnp.dot(mask_field, sin_full, precision=highest)
    spec_real = contract("xk,xj->kj", cos_local, row_real) + contract(
        "xk,xj->kj", sin_local, row_imag
    )
    spec_imag = contract("xk,xj->kj", cos_local, row_imag) - contract(
        "xk,xj->kj", sin_local, row_real
    )
    whole_band = lax.psum(jnp.stack([spec_real, spec_imag], 0), "slab")
    width_here = whole_band.shape[2]
    columns = jnp.arange(width_here, dtype=jnp.int32) - half_band
    passed = pupil_mask(shifted, radius_sq, frequency, columns)
    real_part = passed * whole_band[0][None]
    imag_part = passed * whole_band[1][None]
    lifted_real = contract("xk,skj->sxj", cos_local, real_part) - contract(
        "xk,skj->sxj", sin_local, imag_part
    )
    lifted_imag = contract("xk,skj->sxj", cos_local, imag_part) + contract(
        "xk,skj->sxj", sin_local, real_part
    )
    lifted = jnp.stack([lifted_real, lifted_imag], 1)
    field_real = (
        contract("sxk,yk->sxy", lifted[:, 0], cos_full)
        - contract("sxk,yk->sxy", lifted[:, 1], sin_full)
    ) * norming
    field_imag = (
        contract("sxk,yk->sxy", lifted[:, 0], sin_full)
        + contract("sxk,yk->sxy", lifted[:, 1], cos_full)
    ) * norming
    bright = field_real * field_real + field_imag * field_imag
    onehot_table = (source_groups[:, None] == jnp.arange(NG, dtype=jnp.int32)[None, :]).astype(
        jnp.float32
    )
    weights = jnp.exp(jnp.sum(onehot_table * group_logits[None, :], 1))
    total_weight = jnp.sum(weights)
    weight_share = weights / total_weight
    intensity = jnp.einsum("s,sxy->xy", weight_share, bright, precision=highest)
    resist = jax.nn.sigmoid(steepness * (intensity - threshold))
    misfit = resist - target_print.astype(jnp.float32)
    slope_map = 2.0 * misfit * steepness * resist * (1.0 - resist)
    per_source = contract("sxy,xy->s", bright, slope_map)
    against = jnp.sum(slope_map * intensity)
    squares = jnp.sum(misfit * misfit)
    per_source, against, squares = lax.psum((per_source, against, squares), "slab")
    loss_value = (squares * norming).reshape(1)
    source_pull = weights * (per_source - against) / total_weight
    group_grad = jnp.sum(onehot_table * source_pull[:, None], 0) * norming
    factor = 2.0 * weight_share[:, None, None] * slope_map[None] * norming
    back_real = factor * field_real
    back_imag = factor * field_imag
    down_real = contract("sxy,yk->sxk", back_real, cos_full) + contract(
        "sxy,yk->sxk", back_imag, sin_full
    )
    down_imag = contract("sxy,yk->sxk", back_imag, cos_full) - contract(
        "sxy,yk->sxk", back_real, sin_full
    )
    settle_real = contract("xk,sxj->skj", cos_local, down_real) + contract(
        "xk,sxj->skj", sin_local, down_imag
    )
    settle_imag = contract("xk,sxj->skj", cos_local, down_imag) - contract(
        "xk,sxj->skj", sin_local, down_real
    )
    passed = pupil_mask(shifted, radius_sq, frequency, frequency)
    pull_band = jnp.stack([jnp.sum(passed * settle_real, 0), jnp.sum(passed * settle_imag, 0)], 0)
    whole_pull = lax.psum(pull_band, "slab")
    spread_real = contract("xk,kj->xj", cos_local, whole_pull[0]) - contract(
        "xk,kj->xj", sin_local, whole_pull[1]
    )
    spread_imag = contract("xk,kj->xj", cos_local, whole_pull[1]) + contract(
        "xk,kj->xj", sin_local, whole_pull[0]
    )
    spread_out = jnp.stack([spread_real, spread_imag], 0)
    mask_grad = contract("xk,yk->xy", spread_out[0], cos_full) - contract(
        "xk,yk->xy", spread_out[1], sin_full
    )
    return (loss_value, mask_grad, group_grad)


def solution(mesh):
    in_specs = (
        P(("clip", "slab"), None),
        P(("clip", "slab"), None),
        P("clip", None),
        P("clip"),
        P("clip"),
        P("clip"),
    )
    out_specs = (P("clip"), P(("clip", "slab"), None), P("clip"))
    return jax.shard_map(
        on_device, mesh=mesh, in_specs=in_specs, out_specs=out_specs, check_vma=False
    )
```

profile of v0, /device:TPU:0, one launch (start us, length us, event | category | flops | bytes accessed | tf_op | source)
XLA Modules:
  0.0 627.9 jit_solution(16755961232208500277)
XLA Ops:
  8.4 10.9 %convolution_negate_fusion = f32[256,128]{1,0:T(8,128)S(1)} fusion(f32[128,2048]{1,0:T(8,128)S(1)} %copy-done, s32[256]{0:T(256)S(1)} %iota_add_fusion), kind=kOutput, calls=%fused_computation.93 | convolution fusion | flops 812679168 | bytes 1180672 | tf_op jit(solution)/shard_map/dot_general | solution.py:48
  19.4 11.1 %fusion.112 = f32[256,128]{1,0:T(8,128)S(1)} fusion(f32[128,2048]{1,0:T(8,128)S(1)} %copy-done, s32[256]{0:T(256)S(1)} %iota_add_fusion), kind=kOutput, calls=%fused_computation.110 | convolution fusion | flops 812646400 | bytes 1180672 | tf_op jit(solution)/shard_map/dot_general | solution.py:47
  36.9 92.1 %all-reduce.4.cloned.1.call-done = f32[2,256,256]{2,1,0:T(8,128)} async-done(((f32[2,256,256]{2,1,0:T(8,128)}), f32[2,256,256]{2,1,0:T(8,128)}) %all-reduce.4.cloned.1.call-update) | async-done | bytes 524304 | tf_op jit(solution)/shard_map/psum | solution.py:55
  134.2 5.4 fusion.28
  139.7 6.1 fusion.76
  145.8 37.3 %fusion.41 = f32[16,128,2048]{2,1,0:T(8,128)} fusion(f32[16,256,128]{2,1,0:T(8,128)S(1)} %fusion.76, s32[256]{0:T(256)S(1)} %iota_add_fusion), kind=kOutput, calls=%fused_computation.48 | convolution fusion | flops 12892241920 | bytes 18875392 | tf_op jit(solution)/shard_map/sxk,yk->sxy/dot_general | solution.py:18
  183.2 36.5 %fusion.49 = f32[16,128,2048]{2,1,0:T(8,128)S(1)} fusion(f32[16,256,128]{2,1,0:T(8,128)S(1)} %fusion.76, s32[256]{0:T(256)S(1)} %iota_add_fusion), kind=kOutput, calls=%fused_computation.56 | convolution fusion | flops 12892241920 | bytes 18875392 | tf_op jit(solution)/shard_map/sxk,yk->sxy/dot_general | solution.py:18
  219.7 4.1 fusion.79
  225.2 38.2 %subtract_multiply_fusion = f32[16,128,2048]{2,1,0:T(8,128)} fusion(f32[16,128,2048]{2,1,0:T(8,128)S(1)} %fusion.49, f32[16,256,128]{2,1,0:T(8,128)S(1)} %fusion.79, s32[256]{0:T(256)S(1)} %iota_add_fusion), kind=kOutput, calls=%fused_computation.5 | convolution fusion | flops 12900630528 | bytes 35652608 | tf_op jit(solution)/shard_map/sxk,yk->sxy/dot_general | solution.py:18
  263.4 43.0 %multiply_add_fusion = (f32[16,128,2048]{2,1,0:T(8,128)S(1)}, f32[16,128,2048]{2,1,0:T(8,128)}) fusion(f32[16,128,2048]{2,1,0:T(8,128)} %subtract_multiply_fusion, f32[16,128,2048]{2,1,0:T(8,128)} %fusion.41, s32[256]{0:T(256)S(1)} %iota_add_fusion, f32[16,256,128]{2,1,0:T(8,128)} %copy-done.2), kind=kOutput, calls=%fused_computation.3 | convolution fusion | flops 12913213440 | bytes 69207040 | tf_op jit(solution)/shard_map/sxk,yk->sxy/dot_general | solution.py:18
  306.4 17.7 %fusion.4 = f32[1,128,2048]{2,0,1:T(1,128)S(1)} fusion(f32[16,128,2048]{2,1,0:T(8,128)S(1)} %get-tuple-element.17, f32[]{:T(128)} %exponential_reduce_fusion, f32[16]{0:T(128)S(1)} %select_reduce_fusion.1), kind=kOutput, calls=%fused_computation.8 | convolution fusion | flops 50331664 | bytes 17825860 | tf_op jit(solution)/shard_map/s,sxy->xy/dot_general | solution.py:83
  325.6 25.5 %fusion.94 = f32[16]{0:T(128)} fusion(f32[16,128,2048]{2,1,0:T(8,128)S(1)} %get-tuple-element.17, f32[128,2048,1]{1,0,2:T(8,128)S(1)} %bitcast.127), kind=kOutput, calls=%fused_computation.94 | convolution fusion | flops 50331648 | bytes 17825856 | tf_op jit(solution)/shard_map/sxy,xy->s/dot_general | solution.py:18
  351.1 32.7 %all-reduce = (f32[]{:T(128)}, f32[16]{0:T(128)S(1)}, f32[]{:T(128)}) all-reduce(f32[]{:T(128)} %get-tuple-element.4, f32[16]{0:T(128)} %fusion.94, f32[]{:T(128)} %get-tuple-element.3), channel_id=1, replica_groups=mesh['clip'=2,'slab'=16] {'slab'}, use_global_device_ids=true, to_apply=%region_4.5 | all-reduce | flops 18 | bytes 144 | tf_op jit(solution)/shard_map/psum | solution.py:90
  385.1 25.5 %fusion.6 = f32[16,128,256]{2,1,0:T(8,128)S(1)} fusion(f32[16,128,2048]{2,1,0:T(8,128)} %subtract_multiply_fusion, f32[128,2048]{1,0:T(8,128)S(1)} %get-tuple-element.8, f32[16]{0:T(128)S(1)} %get-tuple-element.16, s32[256]{0:T(256)S(1)} %iota_add_fusion), kind=kOutput, calls=%fused_computation.10 | convolution fusion | flops 12904824832 | bytes 19924032 | tf_op jit(solution)/shard_map/sxy,yk->sxk/dot_general | solution.py:18
  410.6 24.6 %fusion.8 = f32[16,128,256]{2,1,0:T(8,128)S(1)} fusion(f32[16,128,2048]{2,1,0:T(8,128)} %subtract_multiply_fusion, f32[128,2048]{1,0:T(8,128)S(1)} %get-tuple-element.8, f32[16]{0:T(128)S(1)} %get-tuple-element.16, s32[256]{0:T(256)S(1)} %iota_add_fusion), kind=kOutput, calls=%fused_computation.11 | convolution fusion | flops 12904824832 | bytes 19924032 | tf_op jit(solution)/shard_map/sxy,yk->sxk/dot_general | solution.py:18
  435.2 24.9 %fusion.82 = f32[16,128,256]{2,1,0:T(8,128)S(1)} fusion(f32[16,128,256]{2,1,0:T(8,128)S(1)} %fusion.8, f32[16,128,2048]{2,1,0:T(8,128)} %get-tuple-element.18, f32[128,2048]{1,0:T(8,128)S(1)} %get-tuple-element.8, f32[16]{0:T(128)S(1)} %get-tuple-element.16, s32[256]{0:T(256)S(1)} %iota_add_fusion), kind=kOutput, calls=%fused_computation.85 | convolution fusion | flops 12905349120 | bytes 22021184 | tf_op jit(solution)/shard_map/sxy,yk->sxk/dot_general | solution.py:18
  460.1 25.3 %fusion.87 = f32[16,128,256]{2,1,0:T(8,128)S(1)} fusion(f32[16,128,256]{2,1,0:T(8,128)S(1)} %fusion.6, f32[16,128,2048]{2,1,0:T(8,128)} %get-tuple-element.18, f32[128,2048]{1,0:T(8,128)S(1)} %get-tuple-element.8, f32[16]{0:T(128)S(1)} %get-tuple-element.16, s32[256]{0:T(256)S(1)} %iota_add_fusion), kind=kOutput, calls=%fused_computation.86 | convolution fusion | flops 12905349120 | bytes 22021184 | tf_op jit(solution)/shard_map/sxy,yk->sxk/dot_general | solution.py:18
  485.5 4.2 fusion.129
  489.6 4.2 fusion.131
  493.8 5.2 fusion.34
  499.1 5.1 fusion.35
  506.3 86.8 %all-reduce.6.cloned.1.call-done = f32[2,256,256]{1,2,0:T(8,128)} async-done(((f32[2,256,256]{1,2,0:T(8,128)}), f32[2,256,256]{1,2,0:T(8,128)}) %all-reduce.6.cloned.1.call-update) | async-done | bytes 524304 | tf_op jit(solution)/shard_map/psum | solution.py:111
  596.8 9.6 %fusion.109 = f32[128,2048]{1,0:T(8,128)S(1)} fusion(f32[128,256]{1,0:T(8,128)S(1)} %convolution_subtract_fusion.2, s32[256]{0:T(256)S(1)} %iota_add_fusion), kind=kOutput, calls=%fused_computation.109 | convolution fusion | flops 812646400 | bytes 1180672 | tf_op jit(solution)/shard_map/xk,yk->xy/dot_general | solution.py:18
  608.2 11.5 %convolution_subtract_fusion = f32[128,2048]{1,0:T(8,128)} fusion(f32[128,2048]{1,0:T(8,128)S(1)} %fusion.109, f32[128,256]{1,0:T(8,128)S(1)} %convolution_add_fusion.1, s32[256]{0:T(256)S(1)} %iota_add_fusion), kind=kOutput, calls=%fused_computation.42 | convolution fusion | flops 812908544 | bytes 2229248 | tf_op jit(solution)/shard_map/xk,yk->xy/dot_general | solution.py:18
  (55 shorter events, 23.2 us)
Async XLA Ops:
  7.2 1.2 copy-start
  7.2 121.8 %all-reduce.4.cloned.1.call-start = ((), (), s32[]{:S(2)}) async-start(), calls=%async_computation | async-start | bytes 1048576 | tf_op jit(solution)/shard_map/psum | solution.py:55
  30.4 5.6 copy-start.8
  30.4 5.7 copy-start.10
  30.4 5.7 copy-start.11
  35.3 557.8 %all-reduce.6.cloned.1.call-start = ((), (), s32[]{:S(2)}) async-start(), calls=%async_computation.1 | async-start | bytes 1048576 | tf_op jit(solution)/shard_map/psum | solution.py:111
  36.9 182.8 %copy-start.4 = (s32[16,256]{1,0:T(8,128)}, s32[16,256]{1,0:T(8,128)S(1)}, u32[]{:S(2)}) copy-start(s32[16,256]{1,0:T(8,128)S(1)} %get-tuple-element.11) | copy-start | bytes 49156
  36.9 182.8 %copy-start.6 = (s32[16,256]{1,0:T(8,128)}, s32[16,256]{1,0:T(8,128)S(1)}, u32[]{:S(2)}) copy-start(s32[16,256]{1,0:T(8,128)S(1)} %get-tuple-element.12) | copy-start | bytes 49156
  223.9 1.3 copy-start.2
  306.4 17.7 %copy-start.3 = (s32[128,2048]{1,0:T(8,128)S(1)}, s32[128,2048]{1,0:T(8,128)}, u32[]{:S(2)}) copy-start(s32[128,2048]{1,0:T(8,128)} %param.7) | copy-start | bytes 3145732
  489.6 4.2 copy-start.5
  489.6 4.2 copy-start.7
  499.1 5.9 copy-start.12
  596.8 9.6 %copy-start.9 = (f32[2,256,256]{1,2,0:T(8,128)S(1)}, f32[2,256,256]{1,2,0:T(8,128)}, u32[]{:S(2)}) copy-start(f32[2,256,256]{1,2,0:T(8,128)} %all-reduce.6.cloned.1.call-done) | copy-start | bytes 1572868
  608.2 11.5 %copy-start.1 = (f32[128,2048]{1,0:T(8,128)S(1)}, f32[128,2048]{1,0:T(8,128)}, u32[]{:S(2)}) copy-start(f32[128,2048]{1,0:T(8,128)} %param.6) | copy-start | bytes 3145732
Sparse Core Ops, SparseCore 0:
  35.5 93.4 all-reduce.3
  505.1 88.0 all-reduce.5
where the time goes:
time: 637 us; the launch traced here: 628 us
  matrix products  389 us (61%)
  waiting for transfers between devices  179 us (28%)
  blocking collectives  32.7 us (5%)
  between operations  17.1 us (3%)
    dot_general x27, matrix products, contract(): return jnp.einsum(form, left, right, precision=highest)  350 us
    psum x1, waiting for transfers between devices, on_device(): whole_band = lax.psum(jnp.stack([spec_real, spec_imag], 0), 'slab')  92.1 us
    psum x1, waiting for transfers between devices, on_device(): whole_pull = lax.psum(pull_band, 'slab')  86.8 us
    psum x1, blocking collectives, on_device(): lax.psum((per_source, against, squares), 'slab')  32.7 us
    dot_general x1, matrix products, on_device(): intensity = jnp.einsum('s,sxy->xy', weight_share, bright, precision=highest)  17.7 us
  transfers between devices with their start and end apart: 2, of which 2 were waited for; matrix products, arithmetic and copies ran while one was open for 0% of the time, Pallas kernels for 0%

commit v1 on v0

--- a/solution.py
+++ b/solution.py
@@ -108,7 +108,11 @@
     )
     passed = pupil_mask(shifted, radius_sq, frequency, frequency)
     pull_band = jnp.stack([jnp.sum(passed * settle_real, 0), jnp.sum(passed * settle_imag, 0)], 0)
-    whole_pull = lax.psum(pull_band, "slab")
+    whole_pull = pull_band
+    for hop in (1, 2, 4, 8):
+        whole_pull = whole_pull + lax.ppermute(
+            whole_pull, "slab", [(dev, dev ^ hop) for dev in range(16)]
+        )
     spread_real = contract("xk,kj->xj", cos_local, whole_pull[0]) - contract(
         "xk,kj->xj", sin_local, whole_pull[1]
     )

time: 637 us -> 600 us (0.942)
  waiting for transfers between devices: 179 us -> 144 us
    psum x1 -> x0, waiting for transfers between devices: 86.8 us -> none  [on_device(): whole_pull = lax.psum(pull_band, 'slab')]
    ppermute x0 -> x4, waiting for transfers between devices: none -> 52 us  [on_device(): lax.ppermute(whole_pull, 'slab', [(dev, dev ^ hop) for dev in range(16)])]
  transfers between devices with their start and end apart: 2 -> 5, of which waited for: 2 -> 5; matrix products, arithmetic and copies ran while one was open for 0% -> 0% of each run, Pallas kernels for 0% -> 0%
where the time goes in v1:
time: 600 us; the launch traced here: 591 us
  matrix products  387 us (64%)
  waiting for transfers between devices  144 us (24%)
  blocking collectives  32.6 us (5%)
  between operations  17.1 us (3%)
    dot_general x27, matrix products, contract(): return jnp.einsum(form, left, right, precision=highest)  348 us
    psum x1, waiting for transfers between devices, on_device(): whole_band = lax.psum(jnp.stack([spec_real, spec_imag], 0), 'slab')  92.2 us
    ppermute x4, waiting for transfers between devices, on_device(): lax.ppermute(whole_pull, 'slab', [(dev, dev ^ hop) for dev in range(16)])  52 us
    psum x1, blocking collectives, on_device(): lax.psum((per_source, against, squares), 'slab')  32.6 us
    dot_general x1, matrix products, on_device(): intensity = jnp.einsum('s,sxy->xy', weight_share, bright, precision=highest)  17.7 us
  transfers between devices with their start and end apart: 5, of which 5 were waited for; matrix products, arithmetic and copies ran while one was open for 0% of the time, Pallas kernels for 0%

profile of v1, /device:TPU:0, one launch (start us, length us, event | category | flops | bytes accessed | tf_op | source)
XLA Modules:
  0.0 591.0 jit_solution(12933313884918631757)
XLA Ops:
  8.4 10.9 %convolution_negate_fusion = f32[256,128]{1,0:T(8,128)S(1)} fusion(f32[128,2048]{1,0:T(8,128)S(1)} %copy-done, s32[256]{0:T(256)S(1)} %iota_add_fusion), kind=kOutput, calls=%fused_computation.93 | convolution fusion | flops 812679168 | bytes 1180672 | tf_op jit(solution)/shard_map/dot_general | solution.py:48
  19.4 11.1 %fusion.112 = f32[256,128]{1,0:T(8,128)S(1)} fusion(f32[128,2048]{1,0:T(8,128)S(1)} %copy-done, s32[256]{0:T(256)S(1)} %iota_add_fusion), kind=kOutput, calls=%fused_computation.110 | convolution fusion | flops 812646400 | bytes 1180672 | tf_op jit(solution)/shard_map/dot_general | solution.py:47
  36.8 92.2 %all-reduce.3.cloned.1.call-done = f32[2,256,256]{2,1,0:T(8,128)} async-done(((f32[2,256,256]{2,1,0:T(8,128)}), f32[2,256,256]{2,1,0:T(8,128)}) %all-reduce.3.cloned.1.call-update) | async-done | bytes 524304 | tf_op jit(solution)/shard_map/psum | solution.py:55
  134.2 5.4 fusion.28
  139.7 6.1 %fusion.76 = f32[16,256,128]{2,1,0:T(8,128)S(1)} fusion(f32[16,256,128]{2,1,0:T(8,128)} %fusion.28, f32[256,256]{0,1:T(8,128)S(1)} %copy.29, s32[]{:T(128)S(6)} %mul.247, s32[16,256]{1,0:T(8,128)S(1)} %get-tuple-element.12, s32[16,256]{1,0:T(8,128)S(1)} %get-tuple-element.11, s32[256]{0:T(256)S(1)} %iota_add_fusion, s32[128]{0:T(128)S(1)} %iota_add_fusion.1), kind=kOutput, calls=%fused_computation.83 | convolution fusion | flops 1614741504 | bytes 4490756 | tf_op jit(solution)/shard_map/xk,skj->sxj/dot_general | solution.py:18
  145.8 37.3 %fusion.41 = f32[16,128,2048]{2,1,0:T(8,128)} fusion(f32[16,256,128]{2,1,0:T(8,128)S(1)} %fusion.76, s32[256]{0:T(256)S(1)} %iota_add_fusion), kind=kOutput, calls=%fused_computation.48 | convolution fusion | flops 12892241920 | bytes 18875392 | tf_op jit(solution)/shard_map/sxk,yk->sxy/dot_general | solution.py:18
  183.2 36.5 %fusion.49 = f32[16,128,2048]{2,1,0:T(8,128)S(1)} fusion(f32[16,256,128]{2,1,0:T(8,128)S(1)} %fusion.76, s32[256]{0:T(256)S(1)} %iota_add_fusion), kind=kOutput, calls=%fused_computation.56 | convolution fusion | flops 12892241920 | bytes 18875392 | tf_op jit(solution)/shard_map/sxk,yk->sxy/dot_general | solution.py:18
  225.2 38.2 %subtract_multiply_fusion = f32[16,128,2048]{2,1,0:T(8,128)} fusion(f32[16,128,2048]{2,1,0:T(8,128)S(1)} %fusion.49, f32[16,256,128]{2,1,0:T(8,128)S(1)} %fusion.79, s32[256]{0:T(256)S(1)} %iota_add_fusion), kind=kOutput, calls=%fused_computation.5 | convolution fusion | flops 12900630528 | bytes 35652608 | tf_op jit(solution)/shard_map/sxk,yk->sxy/dot_general | solution.py:18
  263.4 43.0 %multiply_add_fusion = (f32[16,128,2048]{2,1,0:T(8,128)S(1)}, f32[16,128,2048]{2,1,0:T(8,128)}) fusion(f32[16,128,2048]{2,1,0:T(8,128)} %subtract_multiply_fusion, f32[16,128,2048]{2,1,0:T(8,128)} %fusion.41, s32[256]{0:T(256)S(1)} %iota_add_fusion, f32[16,256,128]{2,1,0:T(8,128)} %copy-done.2), kind=kOutput, calls=%fused_computation.3 | convolution fusion | flops 12913213440 | bytes 69207040 | tf_op jit(solution)/shard_map/sxk,yk->sxy/dot_general | solution.py:18
  306.4 17.7 %fusion.4 = f32[1,128,2048]{2,0,1:T(1,128)S(1)} fusion(f32[16,128,2048]{2,1,0:T(8,128)S(1)} %get-tuple-element.17, f32[]{:T(128)} %exponential_reduce_fusion, f32[16]{0:T(128)S(1)} %select_reduce_fusion.1), kind=kOutput, calls=%fused_computation.8 | convolution fusion | flops 50331664 | bytes 17825860 | tf_op jit(solution)/shard_map/s,sxy->xy/dot_general | solution.py:83
  325.6 25.5 %fusion.94 = f32[16]{0:T(128)} fusion(f32[16,128,2048]{2,1,0:T(8,128)S(1)} %get-tuple-element.17, f32[128,2048,1]{1,0,2:T(8,128)S(1)} %bitcast.127), kind=kOutput, calls=%fused_computation.94 | convolution fusion | flops 50331648 | bytes 17825856 | tf_op jit(solution)/shard_map/sxy,xy->s/dot_general | solution.py:18
  351.1 32.6 %all-reduce = (f32[]{:T(128)}, f32[16]{0:T(128)S(1)}, f32[]{:T(128)}) all-reduce(f32[]{:T(128)} %get-tuple-element.4, f32[16]{0:T(128)} %fusion.94, f32[]{:T(128)} %get-tuple-element.3), channel_id=1, replica_groups=mesh['clip'=2,'slab'=16] {'slab'}, use_global_device_ids=true, to_apply=%region_4.5 | all-reduce | flops 18 | bytes 144 | tf_op jit(solution)/shard_map/psum | solution.py:90
  385.1 25.5 %fusion.6 = f32[16,128,256]{2,1,0:T(8,128)S(1)} fusion(f32[16,128,2048]{2,1,0:T(8,128)} %subtract_multiply_fusion, f32[128,2048]{1,0:T(8,128)S(1)} %get-tuple-element.8, f32[16]{0:T(128)S(1)} %get-tuple-element.16, s32[256]{0:T(256)S(1)} %iota_add_fusion), kind=kOutput, calls=%fused_computation.10 | convolution fusion | flops 12904824832 | bytes 19924032 | tf_op jit(solution)/shard_map/sxy,yk->sxk/dot_general | solution.py:18
  410.5 24.6 %fusion.8 = f32[16,128,256]{2,1,0:T(8,128)S(1)} fusion(f32[16,128,2048]{2,1,0:T(8,128)} %subtract_multiply_fusion, f32[128,2048]{1,0:T(8,128)S(1)} %get-tuple-element.8, f32[16]{0:T(128)S(1)} %get-tuple-element.16, s32[256]{0:T(256)S(1)} %iota_add_fusion), kind=kOutput, calls=%fused_computation.11 | convolution fusion | flops 12904824832 | bytes 19924032 | tf_op jit(solution)/shard_map/sxy,yk->sxk/dot_general | solution.py:18
  435.2 24.9 %fusion.82 = f32[16,128,256]{2,1,0:T(8,128)S(1)} fusion(f32[16,128,256]{2,1,0:T(8,128)S(1)} %fusion.8, f32[16,128,2048]{2,1,0:T(8,128)} %get-tuple-element.18, f32[128,2048]{1,0:T(8,128)S(1)} %get-tuple-element.8, f32[16]{0:T(128)S(1)} %get-tuple-element.16, s32[256]{0:T(256)S(1)} %iota_add_fusion), kind=kOutput, calls=%fused_computation.85 | convolution fusion | flops 12905349120 | bytes 22021184 | tf_op jit(solution)/shard_map/sxy,yk->sxk/dot_general | solution.py:18
  460.1 25.3 %fusion.87 = f32[16,128,256]{2,1,0:T(8,128)S(1)} fusion(f32[16,128,256]{2,1,0:T(8,128)S(1)} %fusion.6, f32[16,128,2048]{2,1,0:T(8,128)} %get-tuple-element.18, f32[128,2048]{1,0:T(8,128)S(1)} %get-tuple-element.8, f32[16]{0:T(128)S(1)} %get-tuple-element.16, s32[256]{0:T(256)S(1)} %iota_add_fusion), kind=kOutput, calls=%fused_computation.86 | convolution fusion | flops 12905349120 | bytes 22021184 | tf_op jit(solution)/shard_map/sxy,yk->sxk/dot_general | solution.py:18
  485.4 4.2 fusion.129
  493.8 5.2 fusion.34
  499.1 5.1 fusion.35
  506.3 14.0 %collective-permute-done.1 = f32[2,256,256]{1,2,0:T(8,128)S(1)} collective-permute-done((f32[2,256,256]{1,2,0:T(8,128)S(1)}, f32[2,256,256]{1,2,0:T(8,128)S(1)}, u32[]{:S(2)}, u32[]{:S(2)}) %collective-permute-start.1) | collective-permute-done | bytes 524320 | tf_op jit(solution)/shard_map/ppermute | solution.py:113
  520.4 13.1 %collective-permute-done.2 = f32[2,256,256]{1,2,0:T(8,128)S(1)} collective-permute-done((f32[2,256,256]{1,2,0:T(8,128)S(1)}, f32[2,256,256]{1,2,0:T(8,128)S(1)}, u32[]{:S(2)}, u32[]{:S(2)}) %collective-permute-start.2) | collective-permute-done | bytes 524320 | tf_op jit(solution)/shard_map/ppermute | solution.py:113
  535.0 23.1 %collective-permute-done.3 = f32[2,256,256]{1,2,0:T(8,128)S(1)} collective-permute-done((f32[2,256,256]{1,2,0:T(8,128)S(1)}, f32[2,256,256]{1,2,0:T(8,128)S(1)}, u32[]{:S(2)}, u32[]{:S(2)}) %collective-permute-start.3) | collective-permute-done | bytes 524320 | tf_op jit(solution)/shard_map/ppermute | solution.py:113
  561.6 9.6 %fusion.109 = f32[128,2048]{1,0:T(8,128)S(1)} fusion(f32[128,256]{1,0:T(8,128)S(1)} %convolution_subtract_fusion.2, s32[256]{0:T(256)S(1)} %iota_add_fusion), kind=kOutput, calls=%fused_computation.109 | convolution fusion | flops 812646400 | bytes 1180672 | tf_op jit(solution)/shard_map/xk,yk->xy/dot_general | solution.py:18
  571.2 11.5 %convolution_subtract_fusion = f32[128,2048]{1,0:T(8,128)} fusion(f32[128,2048]{1,0:T(8,128)S(1)} %fusion.109, f32[128,256]{1,0:T(8,128)S(1)} %convolution_add_fusion.1, s32[256]{0:T(256)S(1)} %iota_add_fusion), kind=kOutput, calls=%fused_computation.42 | convolution fusion | flops 812908544 | bytes 2229248 | tf_op jit(solution)/shard_map/xk,yk->xy/dot_general | solution.py:18
  (62 shorter events, 31.2 us)
Async XLA Ops:
  7.2 1.2 copy-start
  7.2 121.8 %all-reduce.3.cloned.1.call-start = ((), (), s32[]{:S(2)}) async-start(), calls=%async_computation | async-start | bytes 1048576 | tf_op jit(solution)/shard_map/psum | solution.py:55
  30.4 5.6 copy-start.8
  30.4 5.6 copy-start.9
  30.4 5.6 copy-start.10
  36.8 182.9 %copy-start.4 = (s32[16,256]{1,0:T(8,128)}, s32[16,256]{1,0:T(8,128)S(1)}, u32[]{:S(2)}) copy-start(s32[16,256]{1,0:T(8,128)S(1)} %get-tuple-element.11) | copy-start | bytes 49156
  36.8 182.9 %copy-start.6 = (s32[16,256]{1,0:T(8,128)}, s32[16,256]{1,0:T(8,128)S(1)}, u32[]{:S(2)}) copy-start(s32[16,256]{1,0:T(8,128)S(1)} %get-tuple-element.12) | copy-start | bytes 49156
  223.9 1.3 copy-start.2
  306.4 17.7 %copy-start.3 = (s32[128,2048]{1,0:T(8,128)S(1)}, s32[128,2048]{1,0:T(8,128)}, u32[]{:S(2)}) copy-start(s32[128,2048]{1,0:T(8,128)} %param.7) | copy-start | bytes 3145732
  489.6 4.2 copy-start.5
  489.6 4.2 copy-start.7
  504.2 2.0 collective-permute-start
  506.2 28.1 %copy-start.11 = (s32[16]{0:T(128)S(1)}, s32[16]{0:T(128)}, u32[]{:S(2)}) copy-start(s32[16]{0:T(128)} %param.9) | copy-start | bytes 196
  506.2 14.0 %collective-permute-start.1 = (f32[2,256,256]{1,2,0:T(8,128)S(1)}, f32[2,256,256]{1,2,0:T(8,128)S(1)}, u32[]{:S(2)}, u32[]{:S(2)}) collective-permute-start(f32[2,256,256]{1,2,0:T(8,128)S(1)} %fusion.276), channel_id=1, source_target_pairs={{0,2},{1,3},{2,0},{3,1},{4,6},{5,7},{6,4},{7,5},{8,10},{9,11},{10,... | collective-permute-start | bytes 1572872 | tf_op jit(solution)/shard_map/ppermute | solution.py:113
  520.4 13.2 %collective-permute-start.2 = (f32[2,256,256]{1,2,0:T(8,128)S(1)}, f32[2,256,256]{1,2,0:T(8,128)S(1)}, u32[]{:S(2)}, u32[]{:S(2)}) collective-permute-start(f32[2,256,256]{1,2,0:T(8,128)S(1)} %fusion.289), channel_id=1, source_target_pairs={{0,4},{1,5},{2,6},{3,7},{4,0},{5,1},{6,2},{7,3},{8,12},{9,13},{10,... | collective-permute-start | bytes 1572872 | tf_op jit(solution)/shard_map/ppermute | solution.py:113
  533.6 24.5 %collective-permute-start.3 = (f32[2,256,256]{1,2,0:T(8,128)S(1)}, f32[2,256,256]{1,2,0:T(8,128)S(1)}, u32[]{:S(2)}, u32[]{:S(2)}) collective-permute-start(f32[2,256,256]{1,2,0:T(8,128)S(1)} %add.206), channel_id=1, source_target_pairs={{0,8},{1,9},{2,10},{3,11},{4,12},{5,13},{6,14},{7,15},{8,0},{9,1},... | collective-permute-start | bytes 1572872 | tf_op jit(solution)/shard_map/ppermute | solution.py:113
  571.2 11.5 %copy-start.1 = (f32[128,2048]{1,0:T(8,128)S(1)}, f32[128,2048]{1,0:T(8,128)}, u32[]{:S(2)}) copy-start(f32[128,2048]{1,0:T(8,128)} %param.6) | copy-start | bytes 3145732
Sparse Core Ops, SparseCore 0:
  35.5 93.4 all-reduce.2
